TPU v7x, 256 devices: a whole 4x4x8 slice. The times are simulated.
256 devices in a mesh: ctx: 16 (over y, x), exp: 16 (over z, core).
Axes of the slice: x: 4, y: 4, z: 8, core: 2. Of those that a mesh axis runs over, the one named last changes fastest.
Arguments:
- tokens: bfloat16 [2048, 4096], P('ctx', 'exp'), may hold values from -6 to 6
- input_weight: bfloat16 [4096, 8192], P('ctx', 'exp'), may hold values from -0.09375 to 0.09375
- gate_weight: bfloat16 [4096, 8192], P('ctx', 'exp'), may hold values from -0.09375 to 0.09375
- conv_weight: float32 [4, 8192], P(None, 'exp'), may hold values from -3 to 3
- conv_bias: float32 [8192], P('exp'), may hold values from -3 to 3
- state_weight: bfloat16 [8192, 32], P('exp'), may hold values from -0.0078125 to 0.0078125
- step_size: float32 [2048, 8192], P('ctx', 'exp'), may hold values from 0 to 1, as said below
- skip_gain: float32 [8192], P('exp'), may hold values from 0.5 to 2
- output_weight: bfloat16 [8192, 4096], P('exp', 'ctx'), may hold values from -0.0625 to 0.0625
- norm_gain: float32 [4096], replicated, may hold values from 0.1 to 1.9
- router_weight: bfloat16 [4096, 16], replicated, may hold values from -0.09375 to 0.09375
- expert_gate: bfloat16 [16, 7168, 4096], P('exp', 'ctx'), may hold values from -0.09375 to 0.09375
- expert_up: bfloat16 [16, 7168, 4096], P('exp', 'ctx'), may hold values from -0.09375 to 0.09375
- expert_down: bfloat16 [16, 7168, 4096], P('exp', 'ctx'), may hold values from -0.0625 to 0.0625
- expert_ids: int32 [2048, 2], P(('ctx', 'exp')), may hold values from 0 to 15, all different within a row; in each aligned block of 8 rows (0 to 7, 8 to 15, ...) at most 2 rows name the same one
Outputs:
- layer_out: bfloat16 [2048, 4096], P(('ctx', 'exp'))
Inputs may be any that keep to these rules, and one draw needn't show every extreme that they name: `expert_ids`: each token names 2 different experts; in each aligned block of 8 tokens no expert is named by more than 2 tokens. `step_size`: a positive rate for each token and channel.
All inputs are finite; a program needn't handle non-finite values.
Results may differ from a plain program's by a relative error of at most 0.028.
Values may be sent and summed in bfloat16 or wider, within the bound.
A program may use at most 128 MiB of HBM per device.

v0:
```python
import jax
import jax.numpy as jnp
from jax import lax
from jax.sharding import PartitionSpec as P

STATE = 16
CONV = 4
TOP = 2
CAP = 2
precise = lax.Precision.HIGHEST


def shifted(shard, axis, by):
    devices = lax.axis_size(axis)
    pairs = [(i, i + by) for i in range(devices) if 0 <= i + by < devices]
    return lax.ppermute(shard, axis, pairs)


def running_sum(values):
    length = values.shape[0]
    lower = jnp.tril(jnp.ones((length, length), jnp.float32))
    return jnp.dot(lower, values, precision=precise)


def causal_part(scores, decay_block, input_block):
    length = decay_block.shape[0]
    causal = (jnp.arange(length)[:, None] >= jnp.arange(length)[None, :])[:, :, None]
    distance = decay_block[:, None, :] - decay_block[None, :, :]
    weight = jnp.where(causal, jnp.exp(-jnp.where(causal, distance, 0.0)), 0.0)
    return jnp.einsum("ts,tsc,sc->tc", scores, weight, input_block, precision=precise)


def local(
    tokens,
    input_weight,
    gate_weight,
    conv_weight,
    conv_bias,
    state_weight,
    step_size,
    skip_gain,
    output_weight,
    norm_gain,
    router_weight,
    expert_gate,
    expert_up,
    expert_down,
    expert_ids,
):
    whole_stretch = lax.all_gather(tokens, "exp", axis=1, tiled=True)
    stretch_rows = whole_stretch.shape[0]
    inner_width = input_weight.shape[1]
    inner_x = jnp.dot(
        whole_stretch,
        lax.all_gather(input_weight, "ctx", axis=0, tiled=True),
        preferred_element_type=jnp.float32,
    )
    inner_z = jnp.dot(
        whole_stretch,
        lax.all_gather(gate_weight, "ctx", axis=0, tiled=True),
        preferred_element_type=jnp.float32,
    )
    inner_x = inner_x.astype(jnp.bfloat16)
    inner_z = inner_z.astype(jnp.bfloat16)
    earlier_rows = shifted(inner_x[stretch_rows - (CONV - 1) :], "ctx", 1)
    extended = jnp.concatenate([earlier_rows, inner_x], 0).astype(jnp.float32)
    filtered = jnp.broadcast_to(conv_bias[None, :], (stretch_rows, inner_width))
    for offset in range(CONV):
        filtered = (
            filtered + conv_weight[offset][None, :] * extended[offset : offset + stretch_rows]
        )
    mixer_in = jax.nn.silu(filtered).astype(jnp.bfloat16)
    mixer_wide = mixer_in.astype(jnp.float32)
    projections = lax.psum(
        jnp.dot(mixer_in, state_weight, preferred_element_type=jnp.float32), "exp"
    )
    input_gain = projections[:, :STATE]
    readout = projections[:, STATE:]
    cumulative = running_sum(step_size)
    scores = jnp.dot(readout, input_gain.T, precision=precise)
    block_width = 128
    block_count = inner_width // block_width
    decay_blocks = cumulative.reshape(stretch_rows, block_count, block_width).transpose(1, 0, 2)
    incoming_slabs = mixer_wide.reshape(stretch_rows, block_count, block_width).transpose(1, 0, 2)
    inside = lax.map(
        lambda paired: causal_part(scores, paired[0], paired[1]), (decay_blocks, incoming_slabs)
    )
    inside = inside.transpose(1, 0, 2).reshape(stretch_rows, inner_width)
    total_decay = cumulative[stretch_rows - 1]
    tail_weight = jnp.exp(-(total_decay[None, :] - cumulative)) * mixer_wide
    local_end = jnp.dot(tail_weight.T, input_gain, precision=precise)
    stretch_keep = jnp.exp(-total_decay)

    def relay_step(turn_index, received):
        leaving = stretch_keep[:, None] * received + local_end
        return shifted(leaving, "ctx", 1)

    entering = lax.fori_loop(0, lax.axis_size("ctx") - 1, relay_step, jnp.zeros_like(local_end))
    carried = jnp.exp(-cumulative) * jnp.dot(readout, entering.T, precision=precise)
    mixed_state = (inside + carried + skip_gain[None, :] * mixer_wide) * jax.nn.silu(
        inner_z.astype(jnp.float32)
    )
    blender_result = mixed_state.astype(jnp.bfloat16)
    row_count = expert_ids.shape[0]
    start_row = lax.axis_index("exp") * row_count
    own_tokens = lax.dynamic_slice_in_dim(whole_stretch, start_row, row_count, 0)
    out_whole = lax.all_gather(output_weight, "ctx", axis=1, tiled=True)
    projected = lax.psum_scatter(
        jnp.dot(blender_result, out_whole, preferred_element_type=jnp.float32).astype(jnp.bfloat16),
        "exp",
        scatter_dimension=0,
        tiled=True,
    ).astype(jnp.float32)
    residual = (own_tokens.astype(jnp.float32) + projected).astype(jnp.bfloat16)
    stream = residual.astype(jnp.float32)
    normed = (
        stream
        * lax.rsqrt(jnp.mean(stream * stream, -1, keepdims=True) + 1e-05)
        * norm_gain[None, :]
    ).astype(jnp.bfloat16)
    logits = jnp.dot(normed, router_weight, preferred_element_type=jnp.float32)
    experts = router_weight.shape[1]
    expert_range = jnp.arange(experts, dtype=jnp.int32)
    chosen = expert_ids[:, :, None] == expert_range[None, None, :]
    selected_entry = jnp.sum(jnp.where(chosen, logits[:, None, :], 0.0), -1)
    shares = jax.nn.sigmoid(selected_entry - selected_entry[:, ::-1])
    flat_hits = chosen.reshape(row_count * TOP, experts).astype(jnp.int32)
    earlier_hits = jnp.dot(
        jnp.tril(jnp.ones((row_count * TOP, row_count * TOP), jnp.float32), -1),
        flat_hits.astype(jnp.float32),
        precision=precise,
    ).astype(jnp.int32)
    slot_index = jnp.sum(earlier_hits * flat_hits, -1)
    target = expert_ids.reshape(-1) * CAP + slot_index
    placed = target[:, None] == jnp.arange(experts * CAP, dtype=jnp.int32)[None, :]
    placed = placed.reshape(row_count, TOP, experts * CAP)
    selector = jnp.any(placed, 1).astype(jnp.bfloat16)
    outgoing = lax.dot_general(
        selector, normed, (((0,), (0,)), ((), ())), preferred_element_type=jnp.float32
    ).astype(jnp.bfloat16)
    outgoing = outgoing.reshape(experts, CAP, -1)
    arrived = lax.all_to_all(outgoing, "exp", split_axis=0, concat_axis=0, tiled=True)
    arrived = arrived.reshape(-1, arrived.shape[2])
    gate_part = expert_gate[0]
    up_part = expert_up[0]
    down_part = expert_down[0]
    shard_rows = lax.all_gather(arrived, "ctx", axis=0, tiled=True)
    gate_value = lax.dot_general(
        shard_rows, gate_part, (((1,), (1,)), ((), ())), preferred_element_type=jnp.float32
    )
    up_value = lax.dot_general(
        shard_rows, up_part, (((1,), (1,)), ((), ())), preferred_element_type=jnp.float32
    )
    hidden = (jax.nn.silu(gate_value) * up_value).astype(jnp.bfloat16)
    partial_out = jnp.dot(hidden, down_part, preferred_element_type=jnp.float32)
    finished = lax.psum_scatter(
        partial_out.astype(jnp.bfloat16), "ctx", scatter_dimension=0, tiled=True
    )
    returned = lax.all_to_all(
        finished.reshape(experts, CAP, -1), "exp", split_axis=0, concat_axis=0, tiled=True
    )
    returned = returned.reshape(experts * CAP, -1).astype(jnp.float32)
    combine = jnp.sum(jnp.where(placed, shares[:, :, None], 0.0), 1)
    moe_out = jnp.dot(combine, returned, precision=precise)
    return (stream + moe_out).astype(jnp.bfloat16)


def solution(mesh):
    in_specs = (
        P("ctx", "exp"),
        P("ctx", "exp"),
        P("ctx", "exp"),
        P(None, "exp"),
        P("exp"),
        P("exp", None),
        P("ctx", "exp"),
        P("exp"),
        P("exp", "ctx"),
        P(),
        P(),
        P("exp", "ctx", None),
        P("exp", "ctx", None),
        P("exp", "ctx", None),
        P(("ctx", "exp"), None),
    )
    out_specs = P(("ctx", "exp"), None)
    return jax.shard_map(local, mesh=mesh, in_specs=in_specs, out_specs=out_specs, check_vma=False)
```

profile of v0, /device:TPU:1, one launch (start us, length us, event | category | flops | bytes accessed | tf_op | source)
XLA Modules:
  0.0 636.4 jit_solution(114218375562185634)
XLA Ops:
  6.5 0.7 all-gather.6.cloned.1.call-update
  7.3 0.7 all-gather.8.cloned.1.call-update
  8.1 0.7 all-gather.10.cloned.1.call-update
  8.8 0.5 all-gather.12.cloned.1.call-update
  9.4 0.9 fusion.69
  10.2 0.4 fusion.45
  10.6 40.3 %all-gather.6.cloned.1.call-done = bf16[128,4096]{1,0:T(8,128)(2,1)} async-done(((bf16[128,256]{1,0:T(8,128)(2,1)}), bf16[128,4096]{1,0:T(8,128)(2,1)}) %all-gather.6.cloned.1.call-update) | async-done | bytes 1048592 | tf_op jit(solution)/shard_map/all_gather | solution.py:50
  51.0 57.7 %all-gather.8.cloned.1.call-done = bf16[4096,512]{1,0:T(8,128)(2,1)} async-done(((bf16[256,512]{1,0:T(8,128)(2,1)}), bf16[4096,512]{1,0:T(8,128)(2,1)}) %all-gather.8.cloned.1.call-update) | async-done | bytes 4194320 | tf_op jit(solution)/shard_map/all_gather | solution.py:55
  108.7 3.2 convolution_convert_fusion.4
  112.0 3.1 collective-permute-start.1
  115.1 52.4 %all-gather.10.cloned.1.call-done = bf16[4096,512]{1,0:T(8,128)(2,1)} async-done(((bf16[256,512]{1,0:T(8,128)(2,1)}), bf16[4096,512]{1,0:T(8,128)(2,1)}) %all-gather.10.cloned.1.call-update) | async-done | bytes 4194320 | tf_op jit(solution)/shard_map/all_gather | solution.py:60
  167.4 2.9 fusion.30
  170.7 46.7 %psum.7 = f32[128,32]{0,1:T(8,128)S(1)} all-reduce(f32[128,32]{0,1:T(8,128)S(1)} %fusion.70), channel_id=1, replica_groups=mesh['ctx'=16,'exp'=16] {'exp'}, use_global_device_ids=true, to_apply=%region_0.1 | all-reduce | flops 4096 | bytes 32768 | tf_op jit(solution)/shard_map/psum | solution.py:74
  217.7 0.3 fusion.33
  218.1 39.1 %while.20 = (s32[]{:T(128)}, f32[4,128,128]{2,1,0:T(8,128)S(1)}, f32[4,128,128]{2,1,0:T(8,128)S(1)}, f32[4,128,128]{2,1,0:T(8,128)S(1)}, f32[128,128]{1,0:T(8,128)S(1)}, /*index=5*/s32[]{:T(128)}) while((s32[]{:T(128)}, f32[4,128,128]{2,1,0:T(8,128)S(1)}, f32[4,128,128]{2,1,0:T(8,128)S(1)}, f32[4,128,128]{2,1,0:T(8,128)S(1)}, ...), condition=%wide.region_2.3_spmd, body=%wide.region_1.2_spmd.sunk | while | flops 35667968 | bytes 688205 | solution.py:85
  218.1 9.7 %fusion.104 = f32[128,1,128]{2,1,0:T(1,128)S(1)} fusion(f32[128,128,1]{1,2,0:T(1,128)S(1)} %bitcast.89, f32[128,128]{1,0:T(8,128)S(1)} %get-tuple-element.140, f32[128,128]{1,0:T(8,128)S(1)} %get-tuple-element.141, pred[128,128]{1,0:T(8,128)(4,1)S(1)} %iota_compare_fusion.10), kind=kOutput, calls=%fused_computation.clone.1 | convolution fusion | flops 35651584 | bytes 278528 | tf_op jit(solution)/shard_map/while/body/eval_jaxpr/ts,tsc,sc->tc/dot_general | solution.py:30
  227.9 9.7 %fusion.104 = f32[128,1,128]{2,1,0:T(1,128)S(1)} fusion(f32[128,128,1]{1,2,0:T(1,128)S(1)} %bitcast.89, f32[128,128]{1,0:T(8,128)S(1)} %get-tuple-element.140, f32[128,128]{1,0:T(8,128)S(1)} %get-tuple-element.141, pred[128,128]{1,0:T(8,128)(4,1)S(1)} %iota_compare_fusion.10), kind=kOutput, calls=%fused_computation.clone.1 | convolution fusion | flops 35651584 | bytes 278528 | tf_op jit(solution)/shard_map/while/body/eval_jaxpr/ts,tsc,sc->tc/dot_general | solution.py:30
  237.6 9.7 %fusion.104 = f32[128,1,128]{2,1,0:T(1,128)S(1)} fusion(f32[128,128,1]{1,2,0:T(1,128)S(1)} %bitcast.89, f32[128,128]{1,0:T(8,128)S(1)} %get-tuple-element.140, f32[128,128]{1,0:T(8,128)S(1)} %get-tuple-element.141, pred[128,128]{1,0:T(8,128)(4,1)S(1)} %iota_compare_fusion.10), kind=kOutput, calls=%fused_computation.clone.1 | convolution fusion | flops 35651584 | bytes 278528 | tf_op jit(solution)/shard_map/while/body/eval_jaxpr/ts,tsc,sc->tc/dot_general | solution.py:30
  247.4 9.7 %fusion.104 = f32[128,1,128]{2,1,0:T(1,128)S(1)} fusion(f32[128,128,1]{1,2,0:T(1,128)S(1)} %bitcast.89, f32[128,128]{1,0:T(8,128)S(1)} %get-tuple-element.140, f32[128,128]{1,0:T(8,128)S(1)} %get-tuple-element.141, pred[128,128]{1,0:T(8,128)(4,1)S(1)} %iota_compare_fusion.10), kind=kOutput, calls=%fused_computation.clone.1 | convolution fusion | flops 35651584 | bytes 278528 | tf_op jit(solution)/shard_map/while/body/eval_jaxpr/ts,tsc,sc->tc/dot_general | solution.py:30
  257.1 90.6 %while.21 = (s32[]{:T(128)}, f32[512,16]{0,1:T(8,128)S(1)}, f32[512]{0:T(512)S(1)}, f32[512,16]{0,1:T(8,128)S(1)}, s32[]{:T(128)}) while((s32[]{:T(128)}, f32[512,16]{0,1:T(8,128)S(1)}, f32[512]{0:T(512)S(1)}, f32[512,16]{0,1:T(8,128)S(1)}, s32[]{:T(128)}) %tuple.40), condition=%wide.region_4.5_spmd, body=%wide.region_3.4_spmd.sunk | while | flops 16386 | bytes 231525 | solution.py:98
  257.2 2.7 collective-permute-start
  259.9 1.0 collective-permute-done
  260.9 3.6 collective-permute-start
  264.5 1.0 collective-permute-done
  265.5 3.6 collective-permute-start
  269.2 1.0 collective-permute-done
  270.2 4.0 collective-permute-start
  274.3 1.0 collective-permute-done
  275.3 3.7 collective-permute-start
  279.0 1.0 collective-permute-done
  280.0 5.8 collective-permute-start
  285.8 1.0 collective-permute-done
  286.8 5.7 collective-permute-start
  292.5 1.0 collective-permute-done
  293.5 5.8 collective-permute-start
  299.3 1.0 collective-permute-done
  300.3 5.8 collective-permute-start
  306.1 1.0 collective-permute-done
  307.1 5.8 collective-permute-start
  312.8 1.0 collective-permute-done
  313.8 5.8 collective-permute-start
  319.6 1.0 collective-permute-done
  320.6 5.8 collective-permute-start
  326.4 1.2 collective-permute-done
  327.6 5.6 collective-permute-start
  333.1 1.0 collective-permute-done
  334.2 5.8 collective-permute-start
  339.9 1.0 collective-permute-done
  340.9 5.8 collective-permute-start
  346.7 1.0 collective-permute-done
  347.7 0.5 fusion.29
  348.2 3.9 convolution_convert_fusion.1
  352.9 81.1 %reduce-scatter.3.cloned.1.call-done = bf16[8,4096]{1,0:T(8,128)(2,1)} async-done(((bf16[128,4096]{1,0:T(8,128)(2,1)}), bf16[8,4096]{1,0:T(8,128)(2,1)}) %reduce-scatter.3.cloned.1.call-update) | async-done | bytes 65552 | tf_op jit(solution)/shard_map/reduce_scatter | solution.py:108
  434.0 1.0 fusion.41
  435.4 19.1 %all_to_all.10 = bf16[16,2,4096]{2,1,0:T(2,128)(2,1)S(1)} all-to-all(bf16[16,2,4096]{2,1,0:T(2,128)(2,1)S(1)} %reshape.74), channel_id=1, replica_groups=mesh['ctx'=16,'exp'=16] {'exp'}, dimensions={0} | all-to-all | bytes 524288 | tf_op jit(solution)/shard_map/all_to_all | solution.py:142
  454.5 0.8 reshape.75
  455.6 53.0 %all-gather.14.cloned.1.call-done = bf16[512,4096]{1,0:T(8,128)(2,1)} async-done(((bf16[32,4096]{1,0:T(8,128)(2,1)}), bf16[512,4096]{1,0:T(8,128)(2,1)}) %all-gather.14.cloned.1.call-update) | async-done | bytes 4194320 | tf_op jit(solution)/shard_map/all_gather | solution.py:147
  508.6 5.4 fusion.18
  514.0 10.8 %convolution_convert_fusion = bf16[512,4096]{1,0:T(8,128)(2,1)} fusion(bf16[1,448,4096]{2,1,0:T(8,128)(2,1)} %param.32, bf16[512,4096]{1,0:T(8,128)(2,1)} %all-gather.14.cloned.1.call-done, bf16[1,448,4096]{2,1,0:T(8,128)(2,1)} %param.31, f32[512,448]{0,1:T(8,128)S(1)} %fusion.18), kind=kOutput, calls=%fused_computation.19 | convolution fusion | flops 3761569792 | bytes 16646144 | tf_op jit(solution)/shard_map/dot_general | solution.py:155
  524.8 80.9 %reduce-scatter.5.cloned.1.call-done = bf16[32,4096]{1,0:T(8,128)(2,1)} async-done(((bf16[512,4096]{1,0:T(8,128)(2,1)}), bf16[32,4096]{1,0:T(8,128)(2,1)}) %reduce-scatter.5.cloned.1.call-update) | async-done | bytes 262160 | tf_op jit(solution)/shard_map/reduce_scatter | solution.py:156
  605.7 1.8 reshape.76
  607.5 9.4 %all-to-all-start.1 = ((bf16[16,2,4096]{2,1,0:T(2,128)(2,1)}), bf16[16,2,4096]{2,1,0:T(2,128)(2,1)S(1)}, u32[]{:S(2)}, u32[]{:S(2)}) async-start(bf16[16,2,4096]{2,1,0:T(2,128)(2,1)} %reshape.76), calls=%async_computation.3 | async-start | bytes 524288 | tf_op jit(solution)/shard_map/all_to_all | solution.py:159
  617.4 11.2 %all-to-all-done.1 = bf16[16,2,4096]{2,1,0:T(2,128)(2,1)S(1)} async-done(((bf16[16,2,4096]{2,1,0:T(2,128)(2,1)}), bf16[16,2,4096]{2,1,0:T(2,128)(2,1)S(1)}, u32[]{:S(2)}, u32[]{:S(2)}) %all-to-all-start.1) | async-done | bytes 262176 | tf_op jit(solution)/shard_map/all_to_all | solution.py:159
  628.7 0.9 fusion.14
  (82 shorter events, 3.2 us)
Async XLA Ops:
  6.5 3.7 copy-start
  6.5 44.5 %all-gather.6.cloned.1.call-start = ((), (), s32[]{:S(2)}) async-start(), calls=%async_computation.4 | async-start | bytes 1114112 | tf_op jit(solution)/shard_map/all_gather | solution.py:50
  7.3 101.4 %all-gather.8.cloned.1.call-start = ((), (), s32[]{:S(2)}) async-start(), calls=%async_computation.5 | async-start | bytes 4456448 | tf_op jit(solution)/shard_map/all_gather | solution.py:55
  8.0 159.4 %all-gather.10.cloned.1.call-start = ((), (), s32[]{:S(2)}) async-start(), calls=%async_computation.6 | async-start | bytes 4456448 | tf_op jit(solution)/shard_map/all_gather | solution.py:60
  8.7 339.5 %all-gather.12.cloned.1.call-start = ((), (), s32[]{:S(2)}) async-start(), calls=%async_computation.7 | async-start | bytes 4456448 | tf_op jit(solution)/shard_map/all_gather | solution.py:107
  9.3 424.6 %reduce-scatter.3.cloned.1.call-start = ((), (), s32[]{:S(2)}) async-start(), calls=%async_computation.8 | async-start | bytes 1114112 | tf_op jit(solution)/shard_map/reduce_scatter | solution.py:108
  51.0 116.5 %copy-start.1 = (bf16[128,4096]{1,0:T(8,128)(2,1)S(1)}, bf16[128,4096]{1,0:T(8,128)(2,1)}, u32[]{:S(2)}) copy-start(bf16[128,4096]{1,0:T(8,128)(2,1)} %all-gather.6.cloned.1.call-done) | copy-start | bytes 3145732
  111.9 58.5 %copy-start.5 = (f32[512]{0:T(512)S(1)}, f32[512]{0:T(512)}, u32[]{:S(2)}) copy-start(f32[512]{0:T(512)} %param.23) | copy-start | bytes 6148
  111.9 58.7 %copy-start.2 = (bf16[512,32]{0,1:T(8,128)(2,1)S(1)}, bf16[512,32]{0,1:T(8,128)(2,1)}, u32[]{:S(2)}) copy-start(bf16[512,32]{0,1:T(8,128)(2,1)} %param.24) | copy-start | bytes 98308
  112.0 58.4 %collective-permute-start.1 = (bf16[3,512]{1,0:T(4,128)(2,1)S(1)}, bf16[3,512]{1,0:T(4,128)(2,1)S(1)}, u32[]{:S(2)}, u32[]{:S(2)}) collective-permute-start(bf16[3,512]{1,0:T(4,128)(2,1)S(1)} %slice.48), channel_id=1, source_target_pairs={{0,16},{16,32},{32,48},{48,64},{64,80},{80,96},{96,112},{112,128},... | collective-permute-start | bytes 9224 | tf_op jit(solution)/shard_map/ppermute | solution.py:16
  218.1 129.7 %copy-start.7 = (f32[512]{0:T(512)S(1)}, f32[512]{0:T(512)}, u32[]{:S(2)}) copy-start(f32[512]{0:T(512)} %param.26) | copy-start | bytes 6148
  257.2 3.7 collective-permute-start
  260.9 4.7 collective-permute-start
  265.5 4.7 collective-permute-start
  270.2 5.1 collective-permute-start
  275.3 4.7 collective-permute-start
  280.0 6.9 %collective-permute-start = (f32[512,16]{0,1:T(8,128)S(1)}, f32[512,16]{0,1:T(8,128)S(1)}, u32[]{:S(2)}, u32[]{:S(2)}) collective-permute-start(f32[512,16]{0,1:T(8,128)S(1)} %multiply_add_fusion.3), channel_id=1, source_target_pairs={{0,16},{16,32},{32,48},{48,64},{64,80},{80,96},{96,112},{112,128},... | collective-permute-start | bytes 98312 | tf_op jit(solution)/shard_map/while/body/eval_jaxpr/ppermute | solution.py:16
  286.8 6.7 %collective-permute-start = (f32[512,16]{0,1:T(8,128)S(1)}, f32[512,16]{0,1:T(8,128)S(1)}, u32[]{:S(2)}, u32[]{:S(2)}) collective-permute-start(f32[512,16]{0,1:T(8,128)S(1)} %multiply_add_fusion.3), channel_id=1, source_target_pairs={{0,16},{16,32},{32,48},{48,64},{64,80},{80,96},{96,112},{112,128},... | collective-permute-start | bytes 98312 | tf_op jit(solution)/shard_map/while/body/eval_jaxpr/ppermute | solution.py:16
  293.5 6.8 %collective-permute-start = (f32[512,16]{0,1:T(8,128)S(1)}, f32[512,16]{0,1:T(8,128)S(1)}, u32[]{:S(2)}, u32[]{:S(2)}) collective-permute-start(f32[512,16]{0,1:T(8,128)S(1)} %multiply_add_fusion.3), channel_id=1, source_target_pairs={{0,16},{16,32},{32,48},{48,64},{64,80},{80,96},{96,112},{112,128},... | collective-permute-start | bytes 98312 | tf_op jit(solution)/shard_map/while/body/eval_jaxpr/ppermute | solution.py:16
  300.3 6.8 %collective-permute-start = (f32[512,16]{0,1:T(8,128)S(1)}, f32[512,16]{0,1:T(8,128)S(1)}, u32[]{:S(2)}, u32[]{:S(2)}) collective-permute-start(f32[512,16]{0,1:T(8,128)S(1)} %multiply_add_fusion.3), channel_id=1, source_target_pairs={{0,16},{16,32},{32,48},{48,64},{64,80},{80,96},{96,112},{112,128},... | collective-permute-start | bytes 98312 | tf_op jit(solution)/shard_map/while/body/eval_jaxpr/ppermute | solution.py:16
  307.1 6.8 %collective-permute-start = (f32[512,16]{0,1:T(8,128)S(1)}, f32[512,16]{0,1:T(8,128)S(1)}, u32[]{:S(2)}, u32[]{:S(2)}) collective-permute-start(f32[512,16]{0,1:T(8,128)S(1)} %multiply_add_fusion.3), channel_id=1, source_target_pairs={{0,16},{16,32},{32,48},{48,64},{64,80},{80,96},{96,112},{112,128},... | collective-permute-start | bytes 98312 | tf_op jit(solution)/shard_map/while/body/eval_jaxpr/ppermute | solution.py:16
  313.8 6.8 %collective-permute-start = (f32[512,16]{0,1:T(8,128)S(1)}, f32[512,16]{0,1:T(8,128)S(1)}, u32[]{:S(2)}, u32[]{:S(2)}) collective-permute-start(f32[512,16]{0,1:T(8,128)S(1)} %multiply_add_fusion.3), channel_id=1, source_target_pairs={{0,16},{16,32},{32,48},{48,64},{64,80},{80,96},{96,112},{112,128},... | collective-permute-start | bytes 98312 | tf_op jit(solution)/shard_map/while/body/eval_jaxpr/ppermute | solution.py:16
  320.6 6.9 %collective-permute-start = (f32[512,16]{0,1:T(8,128)S(1)}, f32[512,16]{0,1:T(8,128)S(1)}, u32[]{:S(2)}, u32[]{:S(2)}) collective-permute-start(f32[512,16]{0,1:T(8,128)S(1)} %multiply_add_fusion.3), channel_id=1, source_target_pairs={{0,16},{16,32},{32,48},{48,64},{64,80},{80,96},{96,112},{112,128},... | collective-permute-start | bytes 98312 | tf_op jit(solution)/shard_map/while/body/eval_jaxpr/ppermute | solution.py:16
  327.6 6.6 %collective-permute-start = (f32[512,16]{0,1:T(8,128)S(1)}, f32[512,16]{0,1:T(8,128)S(1)}, u32[]{:S(2)}, u32[]{:S(2)}) collective-permute-start(f32[512,16]{0,1:T(8,128)S(1)} %multiply_add_fusion.3), channel_id=1, source_target_pairs={{0,16},{16,32},{32,48},{48,64},{64,80},{80,96},{96,112},{112,128},... | collective-permute-start | bytes 98312 | tf_op jit(solution)/shard_map/while/body/eval_jaxpr/ppermute | solution.py:16
  334.2 6.8 %collective-permute-start = (f32[512,16]{0,1:T(8,128)S(1)}, f32[512,16]{0,1:T(8,128)S(1)}, u32[]{:S(2)}, u32[]{:S(2)}) collective-permute-start(f32[512,16]{0,1:T(8,128)S(1)} %multiply_add_fusion.3), channel_id=1, source_target_pairs={{0,16},{16,32},{32,48},{48,64},{64,80},{80,96},{96,112},{112,128},... | collective-permute-start | bytes 98312 | tf_op jit(solution)/shard_map/while/body/eval_jaxpr/ppermute | solution.py:16
  340.9 6.8 %collective-permute-start = (f32[512,16]{0,1:T(8,128)S(1)}, f32[512,16]{0,1:T(8,128)S(1)}, u32[]{:S(2)}, u32[]{:S(2)}) collective-permute-start(f32[512,16]{0,1:T(8,128)S(1)} %multiply_add_fusion.3), channel_id=1, source_target_pairs={{0,16},{16,32},{32,48},{48,64},{64,80},{80,96},{96,112},{112,128},... | collective-permute-start | bytes 98312 | tf_op jit(solution)/shard_map/while/body/eval_jaxpr/ppermute | solution.py:16
  347.7 4.5 copy-start.4
  347.7 87.2 %copy-start.3 = (f32[4096]{0:T(1024)S(1)}, f32[4096]{0:T(1024)}, u32[]{:S(2)}) copy-start(f32[4096]{0:T(1024)} %param.28) | copy-start | bytes 49156
  352.1 156.4 %all-gather.14.cloned.1.call-start = ((), (), s32[]{:S(2)}) async-start(), calls=%async_computation.9 | async-start | bytes 4456448 | tf_op jit(solution)/shard_map/all_gather | solution.py:147
  455.3 150.3 %reduce-scatter.5.cloned.1.call-start = ((), (), s32[]{:S(2)}) async-start(), calls=%async_computation.10 | async-start | bytes 4456448 | tf_op jit(solution)/shard_map/reduce_scatter | solution.py:156
  524.8 92.1 %copy-start.6 = (bf16[4096,16]{0,1:T(8,128)(2,1)S(1)}, bf16[4096,16]{0,1:T(8,128)(2,1)}, u32[]{:S(2)}) copy-start(bf16[4096,16]{0,1:T(8,128)(2,1)} %param.29) | copy-start | bytes 393220
  607.5 21.1 %all-to-all-start.1 = ((bf16[16,2,4096]{2,1,0:T(2,128)(2,1)}), bf16[16,2,4096]{2,1,0:T(2,128)(2,1)S(1)}, u32[]{:S(2)}, u32[]{:S(2)}) async-start(bf16[16,2,4096]{2,1,0:T(2,128)(2,1)} %reshape.76), calls=%async_computation.3 | async-start | bytes 524288 | tf_op jit(solution)/shard_map/all_to_all | solution.py:159
Sparse Core Ops, SparseCore 0:
  9.1 41.8 all-gather.5
  53.4 55.2 all-gather.7
  111.1 56.2 all-gather.9
  169.7 61.4 all-gather.11
  352.3 81.6 reduce-scatter.2
  455.4 53.0 all-gather.13
  524.9 80.7 reduce-scatter.4
where the time goes:
time: 637 us; the launch traced here: 636 us
  waiting for transfers between devices  394 us (62%)
  starting transfers between devices  87.9 us (14%)
  matrix products  68.1 us (11%)
  blocking collectives  65.7 us (10%)
  between operations  13.7 us (2%)
    reduce_scatter x1, waiting for transfers between devices, local(): lax.psum_scatter(jnp.dot(blender_result, out_whole, preferred_element_typ...  81.1 us
    reduce_scatter x1, waiting for transfers between devices, local(): lax.psum_scatter(partial_out.astype(jnp.bfloat16), 'ctx', scatter_dimensi...  80.9 us
    ppermute x16, starting transfers between devices, shifted(): return lax.ppermute(shard, axis, pairs)  78.2 us
    all_gather x1, waiting for transfers between devices, local(): lax.all_gather(input_weight, 'ctx', axis=0, tiled=True)  57.7 us
    all_gather x1, waiting for transfers between devices, local(): shard_rows = lax.all_gather(arrived, 'ctx', axis=0, tiled=True)  53 us
    all_gather x1, waiting for transfers between devices, local(): lax.all_gather(gate_weight, 'ctx', axis=0, tiled=True)  52.4 us
    psum x1, blocking collectives, local(): lax.psum(jnp.dot(mixer_in, state_weight, preferred_element_type=jnp.float...  46.7 us
    all_gather x1, waiting for transfers between devices, local(): whole_stretch = lax.all_gather(tokens, 'exp', axis=1, tiled=True)  40.3 us
  transfers between devices with their start and end apart: 24, of which 22 were waited for; matrix products, arithmetic and copies ran while one was open for 8% of the time, Pallas kernels for 0%

commit v1 on v0

--- a/solution.py
+++ b/solution.py
@@ -1,3 +1,4 @@
+import functools
 import jax
 import jax.numpy as jnp
 from jax import lax
@@ -8,6 +9,41 @@
 TOP = 2
 CAP = 2
 precise = lax.Precision.HIGHEST
+
+
+def files_match(point, pos_dim):
+    point = jnp.moveaxis(point, 0, pos_dim)
+    w_next = point.shape
+    return point.reshape(
+        *w_next[:pos_dim], w_next[pos_dim] * w_next[pos_dim + 1], *w_next[pos_dim + 2 :]
+    )
+
+
+def apply_counts(mine_x, axis_name, array_dim):
+    ledger = []
+    width = lax.axis_size(axis_name)
+    for it in range(width):
+        ledger.append((it, (it + 1) % width))
+    trail = []
+    for dev_j, q in ledger:
+        trail.append((q, dev_j))
+    tile_out, clean = ([], [])
+    for ii in range(width - 1):
+        if ii % 2 == 0:
+            tile_out.append(
+                lax.ppermute(tile_out[-1] if tile_out else mine_x, axis_name=axis_name, perm=ledger)
+            )
+        else:
+            clean.append(
+                lax.ppermute(clean[-1] if clean else mine_x, axis_name=axis_name, perm=trail)
+            )
+    tall = jnp.stack([*tile_out[::-1], mine_x, *clean])
+    new = lax.axis_index(axis_name) - len(tile_out)
+    tall = tall[(jnp.arange(width) - new) % width]
+    return files_match(tall, array_dim)
+
+
+run_rings_on = functools.partial(apply_counts, axis_name="ctx", array_dim=0)
 
 
 def shifted(shard, axis, by):
@@ -50,11 +86,7 @@
     whole_stretch = lax.all_gather(tokens, "exp", axis=1, tiled=True)
     stretch_rows = whole_stretch.shape[0]
     inner_width = input_weight.shape[1]
-    inner_x = jnp.dot(
-        whole_stretch,
-        lax.all_gather(input_weight, "ctx", axis=0, tiled=True),
-        preferred_element_type=jnp.float32,
-    )
+    inner_x = jnp.dot(whole_stretch, run_rings_on(input_weight), preferred_element_type=jnp.float32)
     inner_z = jnp.dot(
         whole_stretch,
         lax.all_gather(gate_weight, "ctx", axis=0, tiled=True),

time: 637 us -> 587 us (0.922)
  waiting for transfers between devices: 394 us -> 287 us
  starting transfers between devices: 87.9 us -> 118 us
  local copies, waits for them, and re-layouts: 4.31 us -> 20.9 us
  blocking collectives: 65.7 us -> 75.2 us
    all_gather x1 -> x0, waiting for transfers between devices: 57.7 us -> none  [local(): lax.all_gather(input_weight, 'ctx', axis=0, tiled=True)]
    all_gather x1, waiting for transfers between devices: 52.4 us -> 0.02 us  [local(): lax.all_gather(gate_weight, 'ctx', axis=0, tiled=True)]
    ppermute x0 -> x15, waiting for transfers between devices: none -> 41.3 us  [the longest x8 41.3 us: apply_counts(): lax.ppermute(tile_out[-1] if tile_out else mine_x, axis_name=axis_name, p...]
    all_gather x1, waiting for transfers between devices: 40.3 us -> 0.01 us  [local(): whole_stretch = lax.all_gather(tokens, 'exp', axis=1, tiled=True)]
    ppermute x0 -> x15, starting transfers between devices: none -> 37.3 us  [the longest x7 35.1 us: apply_counts(): lax.ppermute(clean[-1] if clean else mine_x, axis_name=axis_name, perm=tr...]
    unnamed x17 -> x34, local copies, waits for them, and re-layouts: 0.12 us -> 11 us
    psum x1, blocking collectives: 46.7 us -> 56.1 us  [local(): lax.psum(jnp.dot(mixer_in, state_weight, preferred_element_type=jnp.float...]
    ppermute x16, starting transfers between devices: 78.2 us -> 71.4 us  [shifted(): return lax.ppermute(shard, axis, pairs)]
  transfers between devices with their start and end apart: 24 -> 38, of which waited for: 22 -> 28; matrix products, arithmetic and copies ran while one was open for 8% -> 11% of each run, Pallas kernels for 0% -> 0%
where the time goes in v1:
time: 587 us; the launch traced here: 586 us
  waiting for transfers between devices  287 us (49%)
  starting transfers between devices  118 us (20%)
  blocking collectives  75.2 us (13%)
  matrix products  68.2 us (12%)
  local copies, waits for them, and re-layouts  20.9 us (4%)
  between operations  13.8 us (2%)
    reduce_scatter x1, waiting for transfers between devices, local(): lax.psum_scatter(jnp.dot(blender_result, out_whole, preferred_element_typ...  83.1 us
    reduce_scatter x1, waiting for transfers between devices, local(): lax.psum_scatter(partial_out.astype(jnp.bfloat16), 'ctx', scatter_dimensi...  80.9 us
    ppermute x16, starting transfers between devices, shifted(): return lax.ppermute(shard, axis, pairs)  71.4 us
    psum x1, blocking collectives, local(): lax.psum(jnp.dot(mixer_in, state_weight, preferred_element_type=jnp.float...  56.1 us
    all_gather x1, waiting for transfers between devices, local(): shard_rows = lax.all_gather(arrived, 'ctx', axis=0, tiled=True)  53.1 us
    ppermute x8, waiting for transfers between devices, apply_counts(): lax.ppermute(tile_out[-1] if tile_out else mine_x, axis_name=axis_name, p...  41.3 us
    dot_general x4, matrix products, causal_part(): jnp.einsum('ts,tsc,sc->tc', scores, weight, input_block, precision=precise)  38.7 us
    ppermute x7, starting transfers between devices, apply_counts(): lax.ppermute(clean[-1] if clean else mine_x, axis_name=axis_name, perm=tr...  35.1 us
  transfers between devices with their start and end apart: 38, of which 28 were waited for; matrix products, arithmetic and copies ran while one was open for 11% of the time, Pallas kernels for 0%

profile of v1, /device:TPU:1, one launch (start us, length us, event | category | flops | bytes accessed | tf_op | source)
XLA Modules:
  0.0 585.8 jit_solution(6544480303606472909)
XLA Ops:
  8.1 2.1 collective-permute-start.1
  10.2 8.0 %collective-permute-done.1 = bf16[256,512]{1,0:T(8,128)(2,1)S(1)} collective-permute-done((bf16[256,512]{1,0:T(8,128)(2,1)}, bf16[256,512]{1,0:T(8,128)(2,1)S(1)}, u32[]{:S(2)}, u32[]{:S(2)}) %collective-permute-start.1) | collective-permute-done | bytes 262176 | tf_op jit(solution)/shard_map/ppermute | solution.py:34
  18.2 4.8 collective-permute-start.9
  23.0 3.8 collective-permute-done.2
  26.7 5.0 collective-permute-start.10
  31.7 3.5 collective-permute-done.3
  35.3 5.0 collective-permute-start.11
  40.3 3.5 collective-permute-done.4
  43.8 5.0 collective-permute-start.12
  48.8 3.8 collective-permute-done.5
  52.7 5.2 collective-permute-start.13
  57.8 4.6 collective-permute-done.6
  62.8 5.1 collective-permute-start.14
  68.0 8.2 %collective-permute-done.7 = bf16[256,512]{1,0:T(8,128)(2,1)S(1)} collective-permute-done((bf16[256,512]{1,0:T(8,128)(2,1)S(1)}, bf16[256,512]{1,0:T(8,128)(2,1)S(1)}, u32[]{:S(2)}, u32[]{:S(2)}) %collective-permute-start.7) | collective-permute-done | bytes 262176 | tf_op jit(solution)/shard_map/ppermute | solution.py:34
  77.1 5.0 collective-permute-start.15
  82.1 5.9 %collective-permute-done.8 = bf16[256,512]{1,0:T(8,128)(2,1)S(1)} collective-permute-done((bf16[256,512]{1,0:T(8,128)(2,1)S(1)}, bf16[256,512]{1,0:T(8,128)(2,1)S(1)}, u32[]{:S(2)}, u32[]{:S(2)}) %collective-permute-start.8) | collective-permute-done | bytes 262176 | tf_op jit(solution)/shard_map/ppermute | solution.py:34
  99.6 5.0 gather_fusion
  104.6 3.3 fusion.31
  108.0 1.3 collective-permute-start.16
  110.4 56.1 %psum.7 = f32[128,32]{0,1:T(8,128)S(1)} all-reduce(f32[128,32]{0,1:T(8,128)S(1)} %fusion.73), channel_id=1, replica_groups=mesh['ctx'=16,'exp'=16] {'exp'}, use_global_device_ids=true, to_apply=%region_0.1 | all-reduce | flops 4096 | bytes 32768 | tf_op jit(solution)/shard_map/psum | solution.py:106
  167.1 39.1 %while.20 = (s32[]{:T(128)}, f32[4,128,128]{2,1,0:T(8,128)S(1)}, f32[4,128,128]{2,1,0:T(8,128)S(1)}, f32[4,128,128]{2,1,0:T(8,128)S(1)}, f32[128,128]{1,0:T(8,128)S(1)}, /*index=5*/s32[]{:T(128)}) while((s32[]{:T(128)}, f32[4,128,128]{2,1,0:T(8,128)S(1)}, f32[4,128,128]{2,1,0:T(8,128)S(1)}, f32[4,128,128]{2,1,0:T(8,128)S(1)}, ...), condition=%wide.region_2.3_spmd, body=%wide.region_1.2_spmd.sunk | while | flops 35667968 | bytes 688205 | solution.py:117
  167.2 9.7 %fusion.107 = f32[128,1,128]{2,1,0:T(1,128)S(1)} fusion(f32[128,128,1]{1,2,0:T(1,128)S(1)} %bitcast.127, f32[128,128]{1,0:T(8,128)S(1)} %get-tuple-element.140, f32[128,128]{1,0:T(8,128)S(1)} %get-tuple-element.141, pred[128,128]{1,0:T(8,128)(4,1)S(1)} %iota_compare_fusion.10), kind=kOutput, calls=%fused_computation.1.clone.1 | convolution fusion | flops 35651584 | bytes 278528 | tf_op jit(solution)/shard_map/while/body/eval_jaxpr/ts,tsc,sc->tc/dot_general | solution.py:66
  177.0 9.7 %fusion.107 = f32[128,1,128]{2,1,0:T(1,128)S(1)} fusion(f32[128,128,1]{1,2,0:T(1,128)S(1)} %bitcast.127, f32[128,128]{1,0:T(8,128)S(1)} %get-tuple-element.140, f32[128,128]{1,0:T(8,128)S(1)} %get-tuple-element.141, pred[128,128]{1,0:T(8,128)(4,1)S(1)} %iota_compare_fusion.10), kind=kOutput, calls=%fused_computation.1.clone.1 | convolution fusion | flops 35651584 | bytes 278528 | tf_op jit(solution)/shard_map/while/body/eval_jaxpr/ts,tsc,sc->tc/dot_general | solution.py:66
  186.7 9.7 %fusion.107 = f32[128,1,128]{2,1,0:T(1,128)S(1)} fusion(f32[128,128,1]{1,2,0:T(1,128)S(1)} %bitcast.127, f32[128,128]{1,0:T(8,128)S(1)} %get-tuple-element.140, f32[128,128]{1,0:T(8,128)S(1)} %get-tuple-element.141, pred[128,128]{1,0:T(8,128)(4,1)S(1)} %iota_compare_fusion.10), kind=kOutput, calls=%fused_computation.1.clone.1 | convolution fusion | flops 35651584 | bytes 278528 | tf_op jit(solution)/shard_map/while/body/eval_jaxpr/ts,tsc,sc->tc/dot_general | solution.py:66
  196.5 9.7 %fusion.107 = f32[128,1,128]{2,1,0:T(1,128)S(1)} fusion(f32[128,128,1]{1,2,0:T(1,128)S(1)} %bitcast.127, f32[128,128]{1,0:T(8,128)S(1)} %get-tuple-element.140, f32[128,128]{1,0:T(8,128)S(1)} %get-tuple-element.141, pred[128,128]{1,0:T(8,128)(4,1)S(1)} %iota_compare_fusion.10), kind=kOutput, calls=%fused_computation.1.clone.1 | convolution fusion | flops 35651584 | bytes 278528 | tf_op jit(solution)/shard_map/while/body/eval_jaxpr/ts,tsc,sc->tc/dot_general | solution.py:66
  206.2 2.9 fusion.30
  209.2 85.7 %while.21 = (s32[]{:T(128)}, f32[512,16]{0,1:T(8,128)S(1)}, f32[512]{0:T(512)S(1)}, f32[512,16]{0,1:T(8,128)S(1)}, s32[]{:T(128)}) while((s32[]{:T(128)}, f32[512,16]{0,1:T(8,128)S(1)}, f32[512]{0:T(512)S(1)}, f32[512,16]{0,1:T(8,128)S(1)}, s32[]{:T(128)}) %tuple.40), condition=%wide.region_4.5_spmd, body=%wide.region_3.4_spmd.sunk | while | flops 16386 | bytes 231525 | solution.py:130
  209.2 4.3 collective-permute-start
  213.5 1.0 collective-permute-done
  214.5 3.6 collective-permute-start
  218.2 1.0 collective-permute-done
  219.2 3.8 collective-permute-start
  224.0 3.6 collective-permute-start
  228.6 3.6 collective-permute-start
  232.3 1.0 collective-permute-done
  233.3 3.6 collective-permute-start
  237.0 1.0 collective-permute-done
  238.0 3.6 collective-permute-start
  242.6 3.6 collective-permute-start
  246.3 1.0 collective-permute-done
  247.3 5.6 collective-permute-start
  252.9 1.2 collective-permute-done
  254.1 5.6 collective-permute-start
  259.7 1.0 collective-permute-done
  260.7 5.8 collective-permute-start
  266.5 1.0 collective-permute-done
  267.5 5.8 collective-permute-start
  273.3 1.1 collective-permute-done
  274.4 5.7 collective-permute-start
  280.0 1.0 collective-permute-done
  281.0 5.8 collective-permute-start
  286.8 1.0 collective-permute-done
  287.8 6.0 %collective-permute-start = (f32[512,16]{0,1:T(8,128)S(1)}, f32[512,16]{0,1:T(8,128)S(1)}, u32[]{:S(2)}, u32[]{:S(2)}) collective-permute-start(f32[512,16]{0,1:T(8,128)S(1)} %multiply_add_fusion.3), channel_id=1, source_target_pairs={{0,16},{16,32},{32,48},{48,64},{64,80},{80,96},{96,112},{112,128},... | collective-permute-start | bytes 98312 | tf_op jit(solution)/shard_map/while/body/eval_jaxpr/ppermute | solution.py:52
  293.9 1.0 collective-permute-done
  295.4 3.9 convolution_convert_fusion.1
  300.1 83.1 %reduce-scatter.3.cloned.1.call-done = bf16[8,4096]{1,0:T(8,128)(2,1)} async-done(((bf16[128,4096]{1,0:T(8,128)(2,1)}), bf16[8,4096]{1,0:T(8,128)(2,1)}) %reduce-scatter.3.cloned.1.call-update) | async-done | bytes 65552 | tf_op jit(solution)/shard_map/reduce_scatter | solution.py:140
  384.6 19.1 %all_to_all.10 = bf16[16,2,4096]{2,1,0:T(2,128)(2,1)S(1)} all-to-all(bf16[16,2,4096]{2,1,0:T(2,128)(2,1)S(1)} %reshape.127), channel_id=1, replica_groups=mesh['ctx'=16,'exp'=16] {'exp'}, dimensions={0} | all-to-all | bytes 524288 | tf_op jit(solution)/shard_map/all_to_all | solution.py:174
  404.8 53.1 %all-gather.11.cloned.1.call-done = bf16[512,4096]{1,0:T(8,128)(2,1)} async-done(((bf16[32,4096]{1,0:T(8,128)(2,1)}), bf16[512,4096]{1,0:T(8,128)(2,1)}) %all-gather.11.cloned.1.call-update) | async-done | bytes 4194320 | tf_op jit(solution)/shard_map/all_gather | solution.py:179
  457.9 5.4 fusion.18
  463.3 10.8 %convolution_convert_fusion = bf16[512,4096]{1,0:T(8,128)(2,1)} fusion(bf16[1,448,4096]{2,1,0:T(8,128)(2,1)} %param.32, bf16[512,4096]{1,0:T(8,128)(2,1)} %all-gather.11.cloned.1.call-done, bf16[1,448,4096]{2,1,0:T(8,128)(2,1)} %param.31, f32[512,448]{0,1:T(8,128)S(1)} %fusion.18), kind=kOutput, calls=%fused_computation.20 | convolution fusion | flops 3761569792 | bytes 16646144 | tf_op jit(solution)/shard_map/dot_general | solution.py:187
  474.1 80.9 %reduce-scatter.5.cloned.1.call-done = bf16[32,4096]{1,0:T(8,128)(2,1)} async-done(((bf16[512,4096]{1,0:T(8,128)(2,1)}), bf16[32,4096]{1,0:T(8,128)(2,1)}) %reduce-scatter.5.cloned.1.call-update) | async-done | bytes 262160 | tf_op jit(solution)/shard_map/reduce_scatter | solution.py:188
  555.0 1.8 reshape.129
  556.9 9.4 %all-to-all-start.1 = ((bf16[16,2,4096]{2,1,0:T(2,128)(2,1)}), bf16[16,2,4096]{2,1,0:T(2,128)(2,1)S(1)}, u32[]{:S(2)}, u32[]{:S(2)}) async-start(bf16[16,2,4096]{2,1,0:T(2,128)(2,1)} %reshape.129), calls=%async_computation.3 | async-start | bytes 524288 | tf_op jit(solution)/shard_map/all_to_all | solution.py:191
  566.7 11.2 %all-to-all-done.1 = bf16[16,2,4096]{2,1,0:T(2,128)(2,1)S(1)} async-done(((bf16[16,2,4096]{2,1,0:T(2,128)(2,1)}), bf16[16,2,4096]{2,1,0:T(2,128)(2,1)S(1)}, u32[]{:S(2)}, u32[]{:S(2)}) %all-to-all-start.1) | async-done | bytes 262176 | tf_op jit(solution)/shard_map/all_to_all | solution.py:191
  (130 shorter events, 24.6 us)
Async XLA Ops:
  6.5 55.9 %copy-start = (f32[128,512]{1,0:T(8,128)S(1)}, f32[128,512]{1,0:T(8,128)}, u32[]{:S(2)}) copy-start(f32[128,512]{1,0:T(8,128)} %param.25) | copy-start | bytes 786436
  6.5 87.3 %copy-start.2 = (bf16[256,512]{1,0:T(8,128)(2,1)S(1)}, bf16[256,512]{1,0:T(8,128)(2,1)}, u32[]{:S(2)}) copy-start(bf16[256,512]{1,0:T(8,128)(2,1)} %param.20) | copy-start | bytes 786436
  6.5 98.1 %all-gather.5.cloned.1.call-start = ((), (), s32[]{:S(2)}) async-start(), calls=%async_computation.4 | async-start | bytes 1114112 | tf_op jit(solution)/shard_map/all_gather | solution.py:86
  7.3 199.0 %all-gather.7.cloned.1.call-start = ((), (), s32[]{:S(2)}) async-start(), calls=%async_computation.5 | async-start | bytes 4456448 | tf_op jit(solution)/shard_map/all_gather | solution.py:92
  8.0 287.4 %all-gather.9.cloned.1.call-start = ((), (), s32[]{:S(2)}) async-start(), calls=%async_computation.6 | async-start | bytes 4456448 | tf_op jit(solution)/shard_map/all_gather | solution.py:139
  8.1 10.1 %collective-permute-start.1 = (bf16[256,512]{1,0:T(8,128)(2,1)}, bf16[256,512]{1,0:T(8,128)(2,1)S(1)}, u32[]{:S(2)}, u32[]{:S(2)}) collective-permute-start(bf16[256,512]{1,0:T(8,128)(2,1)} %param.20), channel_id=1, source_target_pairs={{0,16},{16,32},{32,48},{48,64},{64,80},{80,96},{96,112},{112,128},... | collective-permute-start | bytes 786440 | tf_op jit(solution)/shard_map/ppermute | solution.py:34
  18.2 8.5 %collective-permute-start.2 = (bf16[256,512]{1,0:T(8,128)(2,1)S(1)}, bf16[256,512]{1,0:T(8,128)(2,1)S(1)}, u32[]{:S(2)}, u32[]{:S(2)}) collective-permute-start(bf16[256,512]{1,0:T(8,128)(2,1)S(1)} %collective-permute-done.1), channel_id=1, source_target_pairs={{0,16},{16,32},{32,48},{48,64},{64,80},{80,96},{96,112},{112,128},... | collective-permute-start | bytes 786440 | tf_op jit(solution)/shard_map/ppermute | solution.py:34
  18.2 8.5 %collective-permute-start.9 = (bf16[256,512]{1,0:T(8,128)(2,1)}, bf16[256,512]{1,0:T(8,128)(2,1)S(1)}, u32[]{:S(2)}, u32[]{:S(2)}) collective-permute-start(bf16[256,512]{1,0:T(8,128)(2,1)} %param.20), channel_id=1, source_target_pairs={{16,0},{32,16},{48,32},{64,48},{80,64},{96,80},{112,96},{128,112},... | collective-permute-start | bytes 786440 | tf_op jit(solution)/shard_map/ppermute | solution.py:38
  26.7 8.5 %collective-permute-start.3 = (bf16[256,512]{1,0:T(8,128)(2,1)S(1)}, bf16[256,512]{1,0:T(8,128)(2,1)S(1)}, u32[]{:S(2)}, u32[]{:S(2)}) collective-permute-start(bf16[256,512]{1,0:T(8,128)(2,1)S(1)} %collective-permute-done.2), channel_id=1, source_target_pairs={{0,16},{16,32},{32,48},{48,64},{64,80},{80,96},{96,112},{112,128},... | collective-permute-start | bytes 786440 | tf_op jit(solution)/shard_map/ppermute | solution.py:34
  26.7 8.5 %collective-permute-start.10 = (bf16[256,512]{1,0:T(8,128)(2,1)S(1)}, bf16[256,512]{1,0:T(8,128)(2,1)S(1)}, u32[]{:S(2)}, u32[]{:S(2)}) collective-permute-start(bf16[256,512]{1,0:T(8,128)(2,1)S(1)} %collective-permute-done.9), channel_id=1, source_target_pairs={{16,0},{32,16},{48,32},{64,48},{80,64},{96,80},{112,96},{128,112},... | collective-permute-start | bytes 786440 | tf_op jit(solution)/shard_map/ppermute | solution.py:38
  35.3 8.5 %collective-permute-start.4 = (bf16[256,512]{1,0:T(8,128)(2,1)S(1)}, bf16[256,512]{1,0:T(8,128)(2,1)S(1)}, u32[]{:S(2)}, u32[]{:S(2)}) collective-permute-start(bf16[256,512]{1,0:T(8,128)(2,1)S(1)} %collective-permute-done.3), channel_id=1, source_target_pairs={{0,16},{16,32},{32,48},{48,64},{64,80},{80,96},{96,112},{112,128},... | collective-permute-start | bytes 786440 | tf_op jit(solution)/shard_map/ppermute | solution.py:34
  35.3 8.5 %collective-permute-start.11 = (bf16[256,512]{1,0:T(8,128)(2,1)S(1)}, bf16[256,512]{1,0:T(8,128)(2,1)S(1)}, u32[]{:S(2)}, u32[]{:S(2)}) collective-permute-start(bf16[256,512]{1,0:T(8,128)(2,1)S(1)} %collective-permute-done.10), channel_id=1, source_target_pairs={{16,0},{32,16},{48,32},{64,48},{80,64},{96,80},{112,96},{128,112},... | collective-permute-start | bytes 786440 | tf_op jit(solution)/shard_map/ppermute | solution.py:38
  43.8 8.8 %collective-permute-start.5 = (bf16[256,512]{1,0:T(8,128)(2,1)S(1)}, bf16[256,512]{1,0:T(8,128)(2,1)S(1)}, u32[]{:S(2)}, u32[]{:S(2)}) collective-permute-start(bf16[256,512]{1,0:T(8,128)(2,1)S(1)} %collective-permute-done.4), channel_id=1, source_target_pairs={{0,16},{16,32},{32,48},{48,64},{64,80},{80,96},{96,112},{112,128},... | collective-permute-start | bytes 786440 | tf_op jit(solution)/shard_map/ppermute | solution.py:34
  43.8 8.8 %collective-permute-start.12 = (bf16[256,512]{1,0:T(8,128)(2,1)S(1)}, bf16[256,512]{1,0:T(8,128)(2,1)S(1)}, u32[]{:S(2)}, u32[]{:S(2)}) collective-permute-start(bf16[256,512]{1,0:T(8,128)(2,1)S(1)} %collective-permute-done.11), channel_id=1, source_target_pairs={{16,0},{32,16},{48,32},{64,48},{80,64},{96,80},{112,96},{128,112},... | collective-permute-start | bytes 786440 | tf_op jit(solution)/shard_map/ppermute | solution.py:38
  52.6 9.8 %collective-permute-start.6 = (bf16[256,512]{1,0:T(8,128)(2,1)S(1)}, bf16[256,512]{1,0:T(8,128)(2,1)S(1)}, u32[]{:S(2)}, u32[]{:S(2)}) collective-permute-start(bf16[256,512]{1,0:T(8,128)(2,1)S(1)} %collective-permute-done.5), channel_id=1, source_target_pairs={{0,16},{16,32},{32,48},{48,64},{64,80},{80,96},{96,112},{112,128},... | collective-permute-start | bytes 786440 | tf_op jit(solution)/shard_map/ppermute | solution.py:34
  52.6 330.5 %reduce-scatter.3.cloned.1.call-start = ((), (), s32[]{:S(2)}) async-start(), calls=%async_computation.7 | async-start | bytes 1114112 | tf_op jit(solution)/shard_map/reduce_scatter | solution.py:140
  52.7 10.1 %collective-permute-start.13 = (bf16[256,512]{1,0:T(8,128)(2,1)S(1)}, bf16[256,512]{1,0:T(8,128)(2,1)S(1)}, u32[]{:S(2)}, u32[]{:S(2)}) collective-permute-start(bf16[256,512]{1,0:T(8,128)(2,1)S(1)} %collective-permute-done.12), channel_id=1, source_target_pairs={{16,0},{32,16},{48,32},{64,48},{80,64},{96,80},{112,96},{128,112},... | collective-permute-start | bytes 786440 | tf_op jit(solution)/shard_map/ppermute | solution.py:38
  62.4 13.8 %collective-permute-start.7 = (bf16[256,512]{1,0:T(8,128)(2,1)S(1)}, bf16[256,512]{1,0:T(8,128)(2,1)S(1)}, u32[]{:S(2)}, u32[]{:S(2)}) collective-permute-start(bf16[256,512]{1,0:T(8,128)(2,1)S(1)} %collective-permute-done.6), channel_id=1, source_target_pairs={{0,16},{16,32},{32,48},{48,64},{64,80},{80,96},{96,112},{112,128},... | collective-permute-start | bytes 786440 | tf_op jit(solution)/shard_map/ppermute | solution.py:34
  62.8 14.3 %collective-permute-start.14 = (bf16[256,512]{1,0:T(8,128)(2,1)S(1)}, bf16[256,512]{1,0:T(8,128)(2,1)S(1)}, u32[]{:S(2)}, u32[]{:S(2)}) collective-permute-start(bf16[256,512]{1,0:T(8,128)(2,1)S(1)} %collective-permute-done.13), channel_id=1, source_target_pairs={{16,0},{32,16},{48,32},{64,48},{80,64},{96,80},{112,96},{128,112},... | collective-permute-start | bytes 786440 | tf_op jit(solution)/shard_map/ppermute | solution.py:38
  76.2 11.8 %collective-permute-start.8 = (bf16[256,512]{1,0:T(8,128)(2,1)S(1)}, bf16[256,512]{1,0:T(8,128)(2,1)S(1)}, u32[]{:S(2)}, u32[]{:S(2)}) collective-permute-start(bf16[256,512]{1,0:T(8,128)(2,1)S(1)} %collective-permute-done.7), channel_id=1, source_target_pairs={{0,16},{16,32},{32,48},{48,64},{64,80},{80,96},{96,112},{112,128},... | collective-permute-start | bytes 786440 | tf_op jit(solution)/shard_map/ppermute | solution.py:34
  77.1 21.8 %collective-permute-start.15 = (bf16[256,512]{1,0:T(8,128)(2,1)S(1)}, bf16[256,512]{1,0:T(8,128)(2,1)S(1)}, u32[]{:S(2)}, u32[]{:S(2)}) collective-permute-start(bf16[256,512]{1,0:T(8,128)(2,1)S(1)} %collective-permute-done.14), channel_id=1, source_target_pairs={{16,0},{32,16},{48,32},{64,48},{80,64},{96,80},{112,96},{128,112},... | collective-permute-start | bytes 786440 | tf_op jit(solution)/shard_map/ppermute | solution.py:38
  104.6 5.4 copy-start.6
  104.6 5.7 copy-start.3
  108.0 2.0 collective-permute-start.16
  167.1 39.1 %copy-start.1 = (bf16[128,4096]{1,0:T(8,128)(2,1)S(1)}, bf16[128,4096]{1,0:T(8,128)(2,1)}, u32[]{:S(2)}) copy-start(bf16[128,4096]{1,0:T(8,128)(2,1)} %all-gather.5.cloned.1.call-done) | copy-start | bytes 3145732
  206.2 88.7 %copy-start.8 = (f32[512]{0:T(512)S(1)}, f32[512]{0:T(512)}, u32[]{:S(2)}) copy-start(f32[512]{0:T(512)} %param.26) | copy-start | bytes 6148
  209.2 5.3 collective-permute-start
  214.5 4.7 collective-permute-start
  219.2 4.8 collective-permute-start
  224.0 4.7 collective-permute-start
  228.6 4.7 collective-permute-start
  233.3 4.7 collective-permute-start
  238.0 4.7 collective-permute-start
  242.6 4.7 collective-permute-start
  247.3 6.8 %collective-permute-start = (f32[512,16]{0,1:T(8,128)S(1)}, f32[512,16]{0,1:T(8,128)S(1)}, u32[]{:S(2)}, u32[]{:S(2)}) collective-permute-start(f32[512,16]{0,1:T(8,128)S(1)} %multiply_add_fusion.3), channel_id=1, source_target_pairs={{0,16},{16,32},{32,48},{48,64},{64,80},{80,96},{96,112},{112,128},... | collective-permute-start | bytes 98312 | tf_op jit(solution)/shard_map/while/body/eval_jaxpr/ppermute | solution.py:52
  254.1 6.6 %collective-permute-start = (f32[512,16]{0,1:T(8,128)S(1)}, f32[512,16]{0,1:T(8,128)S(1)}, u32[]{:S(2)}, u32[]{:S(2)}) collective-permute-start(f32[512,16]{0,1:T(8,128)S(1)} %multiply_add_fusion.3), channel_id=1, source_target_pairs={{0,16},{16,32},{32,48},{48,64},{64,80},{80,96},{96,112},{112,128},... | collective-permute-start | bytes 98312 | tf_op jit(solution)/shard_map/while/body/eval_jaxpr/ppermute | solution.py:52
  260.7 6.8 %collective-permute-start = (f32[512,16]{0,1:T(8,128)S(1)}, f32[512,16]{0,1:T(8,128)S(1)}, u32[]{:S(2)}, u32[]{:S(2)}) collective-permute-start(f32[512,16]{0,1:T(8,128)S(1)} %multiply_add_fusion.3), channel_id=1, source_target_pairs={{0,16},{16,32},{32,48},{48,64},{64,80},{80,96},{96,112},{112,128},... | collective-permute-start | bytes 98312 | tf_op jit(solution)/shard_map/while/body/eval_jaxpr/ppermute | solution.py:52
  267.5 6.9 %collective-permute-start = (f32[512,16]{0,1:T(8,128)S(1)}, f32[512,16]{0,1:T(8,128)S(1)}, u32[]{:S(2)}, u32[]{:S(2)}) collective-permute-start(f32[512,16]{0,1:T(8,128)S(1)} %multiply_add_fusion.3), channel_id=1, source_target_pairs={{0,16},{16,32},{32,48},{48,64},{64,80},{80,96},{96,112},{112,128},... | collective-permute-start | bytes 98312 | tf_op jit(solution)/shard_map/while/body/eval_jaxpr/ppermute | solution.py:52
  274.4 6.7 %collective-permute-start = (f32[512,16]{0,1:T(8,128)S(1)}, f32[512,16]{0,1:T(8,128)S(1)}, u32[]{:S(2)}, u32[]{:S(2)}) collective-permute-start(f32[512,16]{0,1:T(8,128)S(1)} %multiply_add_fusion.3), channel_id=1, source_target_pairs={{0,16},{16,32},{32,48},{48,64},{64,80},{80,96},{96,112},{112,128},... | collective-permute-start | bytes 98312 | tf_op jit(solution)/shard_map/while/body/eval_jaxpr/ppermute | solution.py:52
  281.0 6.8 %collective-permute-start = (f32[512,16]{0,1:T(8,128)S(1)}, f32[512,16]{0,1:T(8,128)S(1)}, u32[]{:S(2)}, u32[]{:S(2)}) collective-permute-start(f32[512,16]{0,1:T(8,128)S(1)} %multiply_add_fusion.3), channel_id=1, source_target_pairs={{0,16},{16,32},{32,48},{48,64},{64,80},{80,96},{96,112},{112,128},... | collective-permute-start | bytes 98312 | tf_op jit(solution)/shard_map/while/body/eval_jaxpr/ppermute | solution.py:52
  287.8 7.1 %collective-permute-start = (f32[512,16]{0,1:T(8,128)S(1)}, f32[512,16]{0,1:T(8,128)S(1)}, u32[]{:S(2)}, u32[]{:S(2)}) collective-permute-start(f32[512,16]{0,1:T(8,128)S(1)} %multiply_add_fusion.3), channel_id=1, source_target_pairs={{0,16},{16,32},{32,48},{48,64},{64,80},{80,96},{96,112},{112,128},... | collective-permute-start | bytes 98312 | tf_op jit(solution)/shard_map/while/body/eval_jaxpr/ppermute | solution.py:52
  294.9 4.5 copy-start.5
  294.9 89.2 %copy-start.4 = (f32[4096]{0:T(1024)S(1)}, f32[4096]{0:T(1024)}, u32[]{:S(2)}) copy-start(f32[4096]{0:T(1024)} %param.28) | copy-start | bytes 49156
  299.3 158.6 %all-gather.11.cloned.1.call-start = ((), (), s32[]{:S(2)}) async-start(), calls=%async_computation.8 | async-start | bytes 4456448 | tf_op jit(solution)/shard_map/all_gather | solution.py:179
  404.5 150.5 %reduce-scatter.5.cloned.1.call-start = ((), (), s32[]{:S(2)}) async-start(), calls=%async_computation.9 | async-start | bytes 4456448 | tf_op jit(solution)/shard_map/reduce_scatter | solution.py:188
  474.1 92.1 %copy-start.7 = (bf16[4096,16]{0,1:T(8,128)(2,1)S(1)}, bf16[4096,16]{0,1:T(8,128)(2,1)}, u32[]{:S(2)}) copy-start(bf16[4096,16]{0,1:T(8,128)(2,1)} %param.29) | copy-start | bytes 393220
  556.9 21.1 %all-to-all-start.1 = ((bf16[16,2,4096]{2,1,0:T(2,128)(2,1)}), bf16[16,2,4096]{2,1,0:T(2,128)(2,1)S(1)}, u32[]{:S(2)}, u32[]{:S(2)}) async-start(bf16[16,2,4096]{2,1,0:T(2,128)(2,1)} %reshape.129), calls=%async_computation.3 | async-start | bytes 524288 | tf_op jit(solution)/shard_map/all_to_all | solution.py:191
Sparse Core Ops, SparseCore 0:
  9.1 41.7 all-gather.4
  53.3 61.6 all-gather.6
  117.4 62.0 all-gather.8
  299.5 83.5 reduce-scatter.2
  404.7 53.1 all-gather.10
  474.3 80.7 reduce-scatter.4
